TPU v7x, 512 devices: a whole 4x4x16 slice. The times are simulated.
512 devices in a mesh: doc: 8 (over y, core), label: 64 (over z, x).
Axes of the slice: x: 4, y: 4, z: 16, core: 2. Of those that a mesh axis runs over, the one named last changes fastest.
Arguments:
- features: float32 [4096, 1024], P('doc'), may hold values from -6 to 6
- doc_labels: int32 [4096, 16], P('doc'), may hold values from 0 to 16383, all different within a row
- tree_perm: int32 [16384], replicated, may hold values from 0 to 16383, as said below
- cluster_sizes: int32 [512], replicated, may hold values from 1 to 4096, 16384 in all
Outputs:
- scores: float32 [4096, 16384], P('doc', 'label')
Inputs may be any that keep to these rules, and one draw needn't show every extreme that they name: `doc_labels`: each document names 16 different labels, and every label is named by some document. `tree_perm`: a permutation; every aligned block of 256 tree positions holds exactly 4 labels of every aligned block of 256 natural indices. `cluster_sizes`: the sizes sum to 16384; the largest is exactly 4096.
All inputs are finite; a program needn't handle non-finite values.
Results may differ from a plain program's by a relative error of at most 0.0001.
Values sent between devices are 32-bit elements; how exact they have to be, the bound alone decides.
No kernel may reach another device: no remote copies, remote signals or barrier semaphores. Data moves between devices by JAX's collectives and lax.ppermute only.
A program may use at most 64 MiB of HBM per device.

v0:
```python
import jax
import jax.numpy as jnp
from jax import lax
from jax.sharding import PartitionSpec as P

L_DEV = 256
EPS = 1e-06


def unit_rows(matrix):
    return matrix * lax.rsqrt(jnp.sum(matrix * matrix, axis=1, keepdims=True) + EPS)


def cluster_of(positions, starts):
    return jnp.sum((starts[None, 1:] <= positions[:, None]).astype(jnp.int32), axis=1)


def shards(features, doc_labels, tree_perm, cluster_sizes):
    width = lax.axis_size("label")
    here = lax.axis_index("label")
    base = here * L_DEV
    slots = jnp.arange(L_DEV, dtype=jnp.int32)
    own_perm = lax.dynamic_slice_in_dim(tree_perm, base, L_DEV)
    incidence = jnp.sum(
        (doc_labels[:, :, None] == own_perm[None, None, :]).astype(jnp.float32), axis=1
    )
    partial_value = lax.dot_general(
        incidence,
        features,
        (((0,), (0,)), ((), ())),
        precision=lax.Precision.HIGHEST,
        preferred_element_type=jnp.float32,
    )
    summed = lax.psum(partial_value, "doc")
    label_rows = unit_rows(summed)
    starts = jnp.cumsum(cluster_sizes) - cluster_sizes
    cluster_ids = cluster_of(base + slots, starts)
    shard = jnp.arange(width, dtype=jnp.int32)
    first_id = cluster_of(shard * L_DEV, starts)
    last_id = cluster_of(shard * L_DEV + (L_DEV - 1), starts)
    same_cluster = (cluster_ids[:, None] == cluster_ids[None, :]).astype(jnp.float32)
    local_sum = jnp.dot(
        same_cluster,
        label_rows,
        precision=lax.Precision.HIGHEST,
        preferred_element_type=jnp.float32,
    )
    ends = jnp.stack([local_sum[0], local_sum[-1]])
    gathered = lax.all_gather(ends, "label").reshape(2 * width, -1)
    other = (shard != here)[None, :]
    take_first = (first_id[None, :] == cluster_ids[:, None]) & other
    take_last = (last_id[None, :] == cluster_ids[:, None]) & (first_id != last_id)[None, :] & other
    weights = jnp.stack([take_first, take_last], axis=2).reshape(L_DEV, 2 * width)
    cluster_sum = local_sum + jnp.dot(
        weights.astype(jnp.float32),
        gathered,
        precision=lax.Precision.HIGHEST,
        preferred_element_type=jnp.float32,
    )
    centroid = unit_rows(cluster_sum)
    combined = label_rows + centroid
    doc_unit = unit_rows(features)
    return lax.dot_general(
        doc_unit,
        combined,
        (((1,), (1,)), ((), ())),
        precision=lax.Precision.HIGHEST,
        preferred_element_type=jnp.float32,
    )


def solution(mesh):
    in_specs = (P("doc", None), P("doc", None), P(), P())
    out_specs = P("doc", "label")
    return jax.shard_map(shards, mesh=mesh, in_specs=in_specs, out_specs=out_specs, check_vma=False)
```

profile of v0, /device:TPU:2, one launch (start us, length us, event | category | flops | bytes accessed | tf_op | source)
XLA Modules:
  0.0 221.0 jit_solution(827182188428001773)
XLA Ops:
  6.5 0.0 all-reduce.2.cloned.1.call-start
  6.5 0.9 copy.11
  7.4 0.8 dynamic_slice.3
  8.2 10.9 %convert_reduce_fusion = f32[512,256]{1,0:T(8,128)S(1)} fusion(s32[256]{0:T(256)S(1)} %dynamic_slice.3, s32[512,16]{1,0:T(8,128)S(1)} %copy.11), kind=kLoop, calls=%fused_computation | loop fusion | flops 6160384 | bytes 558080 | tf_op jit(solution)/shard_map/reduce_sum | solution.py:24
  19.1 0.0 copy-start
  19.1 4.6 %fusion.21 = f32[256,1024]{1,0:T(8,128)} fusion(f32[512,256]{1,0:T(8,128)S(1)} %convert_reduce_fusion, f32[512,1024]{1,0:T(8,128)} %param.4), kind=kOutput, calls=%fused_computation.41 | convolution fusion | flops 1610612736 | bytes 3670016 | tf_op jit(solution)/shard_map/dot_general | solution.py:27
  23.7 0.0 copy-start.2
  23.7 0.0 all-reduce.2.cloned.1.call-update
  23.8 0.0 copy-done
  23.8 0.2 multiply_reduce_fusion
  24.0 0.4 copy-done.2
  24.4 0.3 reduce-window.9
  24.7 0.1 slice.18
  24.8 0.1 slice_reduce_fusion
  24.9 0.1 bitcast_subtract_fusion
  25.0 0.1 slice.20
  25.1 0.2 convert_reduce_fusion.1
  25.3 0.2 convert_reduce_fusion.3
  25.5 0.1 compare_and_fusion
  25.6 80.6 %all-reduce.2.cloned.1.call-done = f32[256,1024]{1,0:T(8,128)} async-done(((f32[256,1024]{1,0:T(8,128)}), f32[256,1024]{1,0:T(8,128)}) %all-reduce.2.cloned.1.call-update) | async-done | bytes 1048592 | tf_op jit(solution)/shard_map/psum | solution.py:34
  106.3 1.4 multiply_reduce_fusion.2
  107.7 2.1 fusion.7
  109.7 0.0 copy-start.1
  109.8 100.7 %all-gather.1 = f32[64,2,1024]{2,1,0:T(2,128)S(1)} all-gather(f32[1,2,1024]{2,1,0:T(2,128)S(1)} %maximum_bitcast_fusion), channel_id=2, replica_groups=mesh['doc'=8,'label'=64] {'label'}, dimensions={0}, use_global_device_ids=true | all-gather | bytes 532480 | tf_op jit(solution)/shard_map/all_gather | solution.py:49
  210.5 0.8 multiply_reduce_fusion.1
  211.4 0.0 copy-done.1
  211.4 2.8 %fusion = f32[512,256]{1,0:T(8,128)} fusion(f32[512,1024]{1,0:T(8,128)S(1)} %copy-done, f32[256,1024]{1,0:T(8,128)S(1)} %get-tuple-element.12, f32[512]{0:T(512)S(1)} %add_rsqrt_fusion, f32[256,1024]{1,0:T(8,128)S(1)} %copy-done.1, f32[256]{0:T(256)S(1)} %add_rsqrt_fusion.1, f32[256]{0:T(256)S(1)} %add_rsqrt_fusion.2), kind=kOutput, calls=%fused_computation.1 | convolution fusion | flops 1611923456 | bytes 4722688 | tf_op jit(solution)/shard_map/dot_general | solution.py:63
  (10 shorter events, 0.1 us)
Async XLA Ops:
  6.5 99.7 %all-reduce.2.cloned.1.call-start = ((), (), s32[]{:S(2)}) async-start(), calls=%async_computation | async-start | bytes 2097152 | tf_op jit(solution)/shard_map/psum | solution.py:34
  19.1 4.7 %copy-start = (f32[512,1024]{1,0:T(8,128)S(1)}, f32[512,1024]{1,0:T(8,128)}, u32[]{:S(2)}) copy-start(f32[512,1024]{1,0:T(8,128)} %param.4) | copy-start | bytes 6291460
  23.7 0.7 copy-start.2
  109.7 101.6 %copy-start.1 = (f32[256,1024]{1,0:T(8,128)S(1)}, f32[256,1024]{1,0:T(8,128)}, u32[]{:S(2)}) copy-start(f32[256,1024]{1,0:T(8,128)} %all-reduce.2.cloned.1.call-done) | copy-start | bytes 3145732
Sparse Core Ops, SparseCore 0:
  23.9 82.3 all-reduce.1
where the time goes:
time: 221 us
  blocking collectives  101 us (46%)
  waiting for transfers between devices  80.6 us (36%)
  between operations  13.5 us (6%)
  other arithmetic  13.4 us (6%)
  matrix products  10.4 us (5%)
  local copies, waits for them, and re-layouts  2.34 us (1%)
    all_gather x1, blocking collectives, shards(): gathered = lax.all_gather(ends, 'label').reshape(2 * width, -1)  101 us
    psum x1, waiting for transfers between devices, shards(): summed = lax.psum(partial_value, 'doc')  80.6 us
    reduce_sum x1, other arithmetic, shards(): jnp.sum((doc_labels[:, :, None] == own_perm[None, None, :]).astype(jnp.fl...  10.9 us
    dot_general x1, matrix products, shards(): lax.dot_general(incidence, features, (((0,), (0,)), ((), ())), precision=...  4.64 us
  transfers between devices with their start and end apart: 1, of which 1 were waited for; matrix products, arithmetic and copies ran while one was open for 1% of the time, Pallas kernels for 0%

commit v1 on v0

--- a/solution.py
+++ b/solution.py
@@ -31,7 +31,7 @@
         precision=lax.Precision.HIGHEST,
         preferred_element_type=jnp.float32,
     )
-    summed = lax.psum(partial_value, "doc")
+    summed = jnp.sum(lax.all_gather(partial_value, "doc"), axis=0)
     label_rows = unit_rows(summed)
     starts = jnp.cumsum(cluster_sizes) - cluster_sizes
     cluster_ids = cluster_of(base + slots, starts)

time: 221 us -> 203 us (0.919)
  the two profiles are of different devices: /device:TPU:2 before, /device:TPU:4 now
where the time goes in v1:
time: 203 us; the launch traced here: 202 us
  blocking collectives  101 us (50%)
  waiting for transfers between devices  60.5 us (30%)
  other arithmetic  16.6 us (8%)
  between operations  13.5 us (7%)
  matrix products  9.18 us (5%)
    all_gather x1, blocking collectives, shards(): gathered = lax.all_gather(ends, 'label').reshape(2 * width, -1)  101 us
    all_gather x1, waiting for transfers between devices, shards(): summed = jnp.sum(lax.all_gather(partial_value, 'doc'), axis=0)  60.5 us
    reduce_sum x1, other arithmetic, shards(): jnp.sum((doc_labels[:, :, None] == own_perm[None, None, :]).astype(jnp.fl...  10.9 us
    dot_general x1, matrix products, shards(): lax.dot_general(incidence, features, (((0,), (0,)), ((), ())), precision=...  4.68 us
    reduce_sum x1, other arithmetic, shards(): summed = jnp.sum(lax.all_gather(partial_value, 'doc'), axis=0)  4.38 us
  transfers between devices with their start and end apart: 1, of which 1 were waited for; matrix products, arithmetic and copies ran while one was open for 1% of the time, Pallas kernels for 0%

profile of v1, /device:TPU:4, one launch (start us, length us, event | category | flops | bytes accessed | tf_op | source)
XLA Modules:
  0.0 202.4 jit_solution(16440744930831291918)
XLA Ops:
  6.5 0.0 all-gather.5.cloned.1.call-start
  6.5 0.9 copy.11
  7.4 0.8 dynamic_slice.3
  8.2 10.9 %convert_reduce_fusion = f32[512,256]{1,0:T(8,128)S(1)} fusion(s32[256]{0:T(256)S(1)} %dynamic_slice.3, s32[512,16]{1,0:T(8,128)S(1)} %copy.11), kind=kLoop, calls=%fused_computation | loop fusion | flops 6160384 | bytes 558080 | tf_op jit(solution)/shard_map/reduce_sum | solution.py:24
  19.1 0.0 copy-start.1
  19.1 0.0 copy-start
  19.1 4.7 %fusion.21 = f32[256,1024]{1,0:T(8,128)} fusion(f32[512,256]{1,0:T(8,128)S(1)} %convert_reduce_fusion, f32[512,1024]{1,0:T(8,128)} %param.4), kind=kOutput, calls=%fused_computation.41 | convolution fusion | flops 1610612736 | bytes 3670016 | tf_op jit(solution)/shard_map/dot_general | solution.py:27
  23.8 0.0 all-gather.5.cloned.1.call-update
  23.8 0.0 copy-done.1
  23.8 0.3 reduce-window.9
  24.1 0.1 slice.18
  24.2 0.1 slice_reduce_fusion
  24.3 0.1 bitcast_subtract_fusion
  24.4 0.1 slice.20
  24.5 0.2 convert_reduce_fusion.3
  24.7 0.2 convert_reduce_fusion.1
  24.9 0.0 copy-done
  24.9 0.2 multiply_reduce_fusion
  25.2 0.1 compare_and_fusion
  25.3 60.5 %all-gather.5.cloned.1.call-done = f32[2048,1024]{1,0:T(8,128)} async-done(((f32[256,1024]{1,0:T(8,128)}), f32[2048,1024]{1,0:T(8,128)}) %all-gather.5.cloned.1.call-update) | async-done | bytes 8388624 | tf_op jit(solution)/shard_map/all_gather | solution.py:34
  85.8 4.4 %reduce_sum.74 = f32[256,1024]{1,0:T(8,128)S(1)} reduce(f32[8,256,1024]{2,1,0:T(8,128)} %bitcast.12, f32[]{:T(128)} %constant.7.clone.1), dimensions={0}, to_apply=%region_2.0 | reduce | flops 1835008 | bytes 9437188 | tf_op jit(solution)/shard_map/reduce_sum | solution.py:34
  90.2 0.1 multiply_reduce_fusion.2
  90.3 0.8 fusion.7
  91.2 100.6 %all-gather.2 = f32[64,2,1024]{2,1,0:T(2,128)S(1)} all-gather(f32[1,2,1024]{2,1,0:T(2,128)S(1)} %maximum_bitcast_fusion), channel_id=3, replica_groups=mesh['doc'=8,'label'=64] {'label'}, dimensions={0}, use_global_device_ids=true | all-gather | bytes 532480 | tf_op jit(solution)/shard_map/all_gather | solution.py:49
  191.8 0.8 multiply_reduce_fusion.1
  192.7 2.8 %fusion = f32[512,256]{1,0:T(8,128)} fusion(f32[512,1024]{1,0:T(8,128)S(1)} %copy-done, f32[256,1024]{1,0:T(8,128)S(1)} %get-tuple-element.12, f32[512]{0:T(512)S(1)} %add_rsqrt_fusion, f32[256,1024]{1,0:T(8,128)S(1)} %reduce_sum.74, f32[256]{0:T(256)S(1)} %add_rsqrt_fusion.1, f32[256]{0:T(256)S(1)} %add_rsqrt_fusion.2), kind=kOutput, calls=%fused_computation.1 | convolution fusion | flops 1611923456 | bytes 4722688 | tf_op jit(solution)/shard_map/dot_general | solution.py:63
  (10 shorter events, 0.1 us)
Async XLA Ops:
  6.5 79.3 %all-gather.5.cloned.1.call-start = ((), (), s32[]{:S(2)}) async-start(), calls=%async_computation | async-start | bytes 9437184 | tf_op jit(solution)/shard_map/all_gather | solution.py:34
  19.1 4.7 %copy-start.1 = (s32[512]{0:T(512)S(1)}, s32[512]{0:T(512)}, u32[]{:S(2)}) copy-start(s32[512]{0:T(512)} %param.7) | copy-start | bytes 6148
  19.1 5.9 %copy-start = (f32[512,1024]{1,0:T(8,128)S(1)}, f32[512,1024]{1,0:T(8,128)}, u32[]{:S(2)}) copy-start(f32[512,1024]{1,0:T(8,128)} %param.4) | copy-start | bytes 6291460
Sparse Core Ops, SparseCore 0:
  23.9 61.8 all-gather.4
